TPU v7x, 256 devices: a whole 4x4x8 slice. The times are simulated.
256 devices in a mesh: row: 32 (over z, x), feat: 8 (over y, core).
Axes of the slice: x: 4, y: 4, z: 8, core: 2. Of those that a mesh axis runs over, the one named last changes fastest.
Arguments:
- bin_codes: int32 [256, 262144], P(None, 'row'), may hold values from 0 to 31
- gradients: bfloat16 [262144], P('row'), may hold values from -6 to 6
- hessians: bfloat16 [262144], P('row'), may hold values from 0.019897461 to 0.25
- pair_list: int32 [64, 2], replicated, may hold values from 0 to 255, as said below
- owners: int32 [64], replicated, may hold values from 0 to 7, as said below
Outputs:
- cut_table: float32 [128, 1024], P('feat', 'row')
- best_gain: float32 [64], replicated
Inputs may be any that keep to these rules, and one draw needn't show every extreme that they name: `pair_list`: each row holds two different features, the first smaller. `owners`: one index owns exactly 16 pairs in every draw, the others at most that many.
All inputs are finite; a program needn't handle non-finite values.
Results may differ from a plain program's by a relative error of at most 0.0003.
Values sent between devices are 32-bit elements; how exact they have to be, the bound alone decides.
A program may use at most 64 MiB of HBM per device.

v0:
```python
import jax
import jax.numpy as jnp
from jax import lax
from jax.sharding import PartitionSpec as P

BINS = 32


LAMBDA_REG = 1.0


def slot_rank(owners):
    pair_ids = jnp.arange(owners.shape[0], dtype=jnp.int32)
    same_owner = owners[:, None] == owners[None, :]
    earlier = pair_ids[None, :] < pair_ids[:, None]
    return jnp.sum((same_owner & earlier).astype(jnp.int32), axis=1)


def cumulate(histogram):
    bin_count = histogram.shape[-2]
    running = jnp.cumsum(histogram, axis=-2)
    shaped = running.reshape(running.shape[:-1] + (2, bin_count))
    shaped = jnp.cumsum(shaped, axis=-1)
    return shaped.reshape(running.shape)


def cut_gains(cut_rows, margin_row):
    bin_count = margin_row.shape[-1] // 2
    grad_cum = cut_rows[..., :bin_count]
    hess_cum = cut_rows[..., bin_count:]
    grad_end = grad_cum[..., -1:]
    hess_end = hess_cum[..., -1:]
    grad_col = margin_row[..., None, :bin_count]
    hess_col = margin_row[..., None, bin_count:]
    grad_all = margin_row[..., None, bin_count - 1 : bin_count]
    hess_all = margin_row[..., None, 2 * bin_count - 1 :]
    quad_grad = (
        grad_cum,
        grad_end - grad_cum,
        grad_col - grad_cum,
        grad_all - grad_end - grad_col + grad_cum,
    )
    quad_hess = (
        hess_cum,
        hess_end - hess_cum,
        hess_col - hess_cum,
        hess_all - hess_end - hess_col + hess_cum,
    )
    result = -(grad_all * grad_all) / (hess_all + LAMBDA_REG)
    for grad_part, hess_part in zip(quad_grad, quad_hess):
        result = result + grad_part * grad_part / (hess_part + LAMBDA_REG)
    return result


def shards(bin_codes, gradients, hessians, pair_list, owners):
    feat_count = lax.axis_size("feat")
    row_count = lax.axis_size("row")
    feat_index = lax.axis_index("feat")
    row_index = lax.axis_index("row")
    pair_count = pair_list.shape[0]
    bin_count = BINS
    row_share = bin_count // row_count
    home_slots = 2 * pair_count // feat_count
    rank = slot_rank(owners)
    pair_ids = jnp.arange(pair_count, dtype=jnp.int32)
    places = jnp.arange(home_slots, dtype=jnp.int32)
    matched = (owners[None, :] == feat_index) & (rank[None, :] == places[:, None])
    chosen = jnp.sum(jnp.where(matched, pair_ids[None, :], 0), axis=1)
    present = jnp.any(matched, axis=1)
    lookup = owners * home_slots + rank
    chosen_pairs = pair_list[chosen]
    picked = jnp.take(bin_codes, chosen_pairs.reshape(-1), axis=0)
    picked = picked.reshape(home_slots, 2, -1)
    levels = jnp.arange(bin_count, dtype=jnp.int32)
    hot_first = (picked[:, 0, None, :] == levels[None, :, None]).astype(jnp.bfloat16)
    hot_second = (picked[:, 1, None, :] == levels[None, :, None]).astype(jnp.bfloat16)
    weighted = jnp.concatenate(
        [hot_second * gradients[None, None, :], hot_second * hessians[None, None, :]], axis=1
    )
    histogram = jnp.einsum("sar,sxr->sax", hot_first, weighted, preferred_element_type=jnp.float32)
    histogram = histogram * present[:, None, None].astype(jnp.float32)
    summed = lax.psum(histogram, "row")
    running = cumulate(summed)
    cut_rows = lax.dynamic_slice_in_dim(running, row_index * row_share, row_share, 1)
    margin_row = running[:, -1, :]
    cut_gain = cut_gains(cut_rows, margin_row).reshape(home_slots, row_share * bin_count)
    row_peak = lax.pmax(jnp.max(cut_gain, axis=1), "row")
    everyone = lax.all_gather(row_peak, "feat", axis=0, tiled=True)
    best_gain = everyone[lookup]
    return (cut_gain, best_gain)


def solution(mesh):
    in_specs = (P(None, "row"), P("row"), P("row"), P(), P())
    out_specs = (P("feat", "row"), P())
    return jax.shard_map(shards, mesh=mesh, in_specs=in_specs, out_specs=out_specs, check_vma=False)
```

profile of v0, /device:TPU:1, one launch (start us, length us, event | category | flops | bytes accessed | tf_op | source)
XLA Modules:
  0.0 291.0 jit_solution(3564876768124046581)
XLA Ops:
  7.2 0.0 copy-start
  7.2 0.0 copy-start.1
  7.2 0.0 all-reduce.3.cloned.1.call-start
  7.2 0.9 convert_reduce_fusion
  8.1 0.7 broadcast_compare_fusion
  8.8 0.1 select_reduce_fusion
  9.0 0.8 copy.58
  9.7 0.6 gather_fusion
  10.3 0.1 reshape.114
  10.4 0.1 fusion.23
  10.5 4.7 %gather_fusion.1 = s32[32,8192]{1,0:T(8,128)S(1)} fusion(s32[256,8192]{1,0:T(8,128)} %param.5, s32[1024]{0:T(1024)S(1)} %pad_clamp_fusion.1), kind=kCustom, calls=%fused_computation.1 | custom fusion | bytes 2097280 | tf_op jit(solution)/shard_map/jit(_take)/gather | solution.py:72
  15.3 0.6 gather.14
  15.9 0.1 copy.59
  16.0 0.7 copy_select_fusion
  16.7 0.1 slice_bitcast_fusion.1
  16.8 0.0 copy-done
  16.8 0.0 copy-done.1
  16.8 9.2 %fusion.5 = (bf16[16,32,8192]{2,1,0:T(8,128)(2,1)}, bf16[16,32,8192]{2,1,0:T(8,128)(2,1)}) fusion(s32[16,8192]{1,0:T(8,128)S(1)} %get-tuple-element.11, bf16[8192]{0:T(1024)(128)(2,1)S(1)} %copy-done, bf16[8192]{0:T(1024)(128)(2,1)S(1)} %copy-done.1), kind=kLoop, calls=%fused_computation.9 | loop fusion | flops 12582912 | bytes 17334272 | tf_op jit(solution)/shard_map/mul | solution.py:78
  26.0 0.0 copy-start.2
  26.0 0.0 copy-start.3
  26.0 8.4 %fusion.7 = f32[16,32,64]{2,1,0:T(8,128)S(1)} fusion(bf16[16,32,8192]{2,1,0:T(8,128)(2,1)} %get-tuple-element.13, bf16[16,32,8192]{2,1,0:T(8,128)(2,1)} %get-tuple-element.12, s32[16,8192]{1,0:T(8,128)S(1)} %get-tuple-element.10, f32[16]{0:T(128)S(1)} %convert_element_type.14), kind=kOutput, calls=%fused_computation.12 | convolution fusion | flops 574652416 | bytes 17432640 | tf_op jit(solution)/shard_map/sar,sxr->sax/dot_general | solution.py:80
  34.3 0.3 reduce_window_sum.24
  34.7 1.1 copy.61
  35.8 0.0 all-reduce.3.cloned.1.call-update
  35.8 0.0 copy-done.2
  35.8 0.0 copy-done.3
  35.8 0.6 dynamic-slice
  37.1 146.9 %all-reduce.3.cloned.1.call-done = f32[16,32,2,32]{3,0,1,2:T(8,128)} async-done(((f32[16,32,2,32]{3,0,1,2:T(8,128)}), f32[16,32,2,32]{3,0,1,2:T(8,128)}) %all-reduce.3.cloned.1.call-update) | async-done | bytes 131088 | tf_op jit(solution)/shard_map/psum | solution.py:82
  184.0 1.1 fusion.29
  185.1 0.2 copy.62
  185.2 6.1 %reduce_window_sum.26 = f32[16,32,2,32]{3,1,2,0:T(8,128)S(1)} reduce-window(f32[16,32,2,32]{3,1,2,0:T(8,128)S(1)} %copy.62, f32[]{:T(128)} %constant.45.clone.1), window={size=1x1x1x32 pad=0_0x0_0x0_0x31_0}, to_apply=%region_5.6 | reduce-window | flops 1015808 | bytes 262148 | tf_op jit(solution)/shard_map/jit(cumsum)/reduce_window_sum | solution.py:23
  191.4 0.4 copy.68
  191.8 0.3 reshape.147
  192.1 0.2 fusion.21
  192.3 0.2 fusion.16
  192.5 0.8 fusion.27
  193.3 58.4 %pmax.7 = f32[16]{0:T(128)S(1)} all-reduce(f32[16]{0:T(128)S(1)} %get-tuple-element.8), channel_id=1, replica_groups=mesh['row'=32,'feat'=8] {'row'}, use_global_device_ids=true, to_apply=%region_7.8 | all-reduce | flops 16 | bytes 128 | tf_op jit(solution)/shard_map/pmax | solution.py:87
  251.8 0.2 dynamic-update-slice
  252.0 30.9 %all-reduce = f32[128]{0:T(128)S(1)} all-reduce(f32[128]{0:T(128)S(1)} %dynamic-update-slice), channel_id=1, replica_groups=mesh['row'=32,'feat'=8] {'feat'}, use_global_device_ids=true, to_apply=%add | all-reduce | flops 128 | bytes 1024
  282.9 1.3 gather_fusion.2
  (10 shorter events, 0.1 us)
Async XLA Ops:
  7.2 9.6 %copy-start = (bf16[8192]{0:T(1024)(128)(2,1)S(1)}, bf16[8192]{0:T(1024)(128)(2,1)}, u32[]{:S(2)}) copy-start(bf16[8192]{0:T(1024)(128)(2,1)} %param.6) | copy-start | bytes 49156
  7.2 9.6 %copy-start.1 = (bf16[8192]{0:T(1024)(128)(2,1)S(1)}, bf16[8192]{0:T(1024)(128)(2,1)}, u32[]{:S(2)}) copy-start(bf16[8192]{0:T(1024)(128)(2,1)} %param.7) | copy-start | bytes 49156
  7.2 176.8 %all-reduce.3.cloned.1.call-start = ((), (), s32[]{:S(2)}) async-start(), calls=%async_computation | async-start | bytes 1048576 | tf_op jit(solution)/shard_map/psum | solution.py:82
  26.0 9.8 %copy-start.2 = (s32[64]{0:T(128)S(1)}, s32[64]{0:T(128)}, u32[]{:S(2)}) copy-start(s32[64]{0:T(128)} %param.9) | copy-start | bytes 772
  26.0 9.9 %copy-start.3 = (u32[256]{0:T(256)S(1)}, u32[256]{0:T(256)}, u32[]{:S(2)}) copy-start(u32[256]{0:T(256)} %constant.55) | copy-start | bytes 3076
Sparse Core Ops, SparseCore 0:
  35.9 148.0 all-reduce.2
where the time goes:
time: 291 us
  waiting for transfers between devices  147 us (51%)
  blocking collectives  89.3 us (31%)
  other arithmetic  20.2 us (7%)
  between operations  14.9 us (5%)
  local copies, waits for them, and re-layouts  11.4 us (4%)
  matrix products  8.35 us (3%)
    psum x1, waiting for transfers between devices, shards(): summed = lax.psum(histogram, 'row')  147 us
    pmax x1, blocking collectives, shards(): row_peak = lax.pmax(jnp.max(cut_gain, axis=1), 'row')  58.4 us
    unnamed x1, blocking collectives  30.9 us
    mul x1, other arithmetic, shards(): hot_second * gradients[None, None, :]  9.18 us
    dot_general x1, matrix products, shards(): jnp.einsum('sar,sxr->sax', hot_first, weighted, preferred_element_type=jn...  8.35 us
    another operation x1, other arithmetic, cumulate(): shaped = jnp.cumsum(shaped, axis=-1)  6.13 us
  transfers between devices with their start and end apart: 1, of which 1 were waited for; matrix products, arithmetic and copies ran while one was open for 0% of the time, Pallas kernels for 0%

commit v1 on v0

v1 whole, which is shorter than its diff:
```python
import jax
import jax.numpy as jnp
from jax import lax
from jax.experimental import pallas as pl
from jax.experimental.pallas import tpu as pltpu
from jax.sharding import PartitionSpec as P

BINS = 32
LAMBDA_REG = 1.0
ROW = 32
FEAT = 8
PAIRS = 8
CHUNKS = 4
STEP = 1024
MESH = pl.DeviceIdType.MESH


def kernel(pairs_ref, owners_ref, grad_ref, hess_ref, codes_hbm, table_ref, best_ref,
           codes_0, codes_1, codes_2, codes_3, acc, send, recv, gains, peak, peaks,
           code_sem, sum_send, sum_recv, gain_send, gain_recv, peak_send, peak_recv):
    row = lax.axis_index("row")
    feat = lax.axis_index("feat")
    chunks = (codes_0, codes_1, codes_2, codes_3)
    chunk_width = codes_0.shape[1]
    width = STEP

    def fetch(c):
        lanes = pl.ds(c * chunk_width, chunk_width)
        return pltpu.make_async_copy(codes_hbm.at[:, lanes], chunks[c], code_sem.at[c])

    for c in range(CHUNKS):
        fetch(c).start()

    barrier = pltpu.get_barrier_semaphore()

    @pl.loop(1, ROW)
    def _(k):
        other = lax.rem(row + k, ROW)
        pl.semaphore_signal(barrier, inc=1, device_id=(other, feat), device_id_type=MESH)

    @pl.loop(1, FEAT)
    def _(k):
        other = lax.rem(feat + k, FEAT)
        pl.semaphore_signal(barrier, inc=1, device_id=(row, other), device_id_type=MESH)

    acc[...] = jnp.zeros_like(acc)
    level = lax.broadcasted_iota(jnp.int32, (16, width), 0).astype(jnp.float32).astype(jnp.bfloat16)
    level_up = level + jnp.bfloat16(16)
    one = jnp.ones((16, width), jnp.bfloat16)
    zero = jnp.zeros((16, width), jnp.bfloat16)
    sub = width // 128

    def accumulate(c, codes, inner):
        start = pl.multiple_of(inner * width, width)
        block = c * (chunk_width // width) + inner

        def spread(ref):
            rows = ref[pl.ds(pl.multiple_of(block * sub, sub), sub), :].astype(jnp.float32)
            flat = jnp.concatenate([rows[j:j + 1, :] for j in range(sub)], axis=1)
            return jnp.broadcast_to(flat, (16, width)).astype(jnp.bfloat16)

        grad = spread(grad_ref)
        hess = spread(hess_ref)
        for group in range(2):
            first, second = [], []
            for i in range(4):
                p = feat * PAIRS + group * 4 + i
                ca = codes[pl.ds(pairs_ref[0, p], 1), pl.ds(start, width)].astype(jnp.float32)
                cb = codes[pl.ds(pairs_ref[1, p], 1), pl.ds(start, width)].astype(jnp.float32)
                ca = jnp.broadcast_to(ca, (16, width)).astype(jnp.bfloat16)
                cb = jnp.broadcast_to(cb, (16, width)).astype(jnp.bfloat16)
                first += [jnp.where(ca <= level, one, zero), jnp.where(ca <= level_up, one, zero)]
                low, high = cb <= level, cb <= level_up
                second += [jnp.where(low, grad, zero), jnp.where(high, grad, zero),
                           jnp.where(low, hess, zero), jnp.where(high, hess, zero)]
            lhs = jnp.concatenate(first, axis=0)
            rhs = jnp.concatenate(second, axis=0)
            acc[group] += lax.dot_general(lhs, rhs, (((1,), (1,)), ((), ())),
                                          preferred_element_type=jnp.float32)

    for c in range(CHUNKS):
        fetch(c).wait()

        @pl.loop(0, chunk_width // width)
        def _(inner):
            accumulate(c, chunks[c], inner)

    for p in range(PAIRS):
        group, i = p // 4, p % 4
        block = acc[group, 32 * i:32 * i + 32, 64 * i:64 * i + 64]
        last = jnp.broadcast_to(block[31:32, :], (BINS, 64))
        send[:, p, :] = jnp.concatenate([block, last], axis=1)

    mine = owners_ref[...] == feat
    mine_value = jnp.where(mine, 1.0, 0.0).astype(jnp.bfloat16)
    before = lax.broadcasted_iota(jnp.int32, (64, 64), 0) < lax.broadcasted_iota(jnp.int32, (64, 64), 1)
    rank = jnp.dot(mine_value, jnp.where(before, 1.0, 0.0).astype(jnp.bfloat16),
                   preferred_element_type=jnp.float32)
    slot = lax.broadcasted_iota(jnp.int32, (16, 64), 0).astype(jnp.float32)
    chosen = jnp.where((jnp.broadcast_to(rank, (16, 64)) == slot) & jnp.broadcast_to(mine, (16, 64)), 1.0, 0.0)

    pl.semaphore_wait(barrier, ROW - 1 + FEAT - 1)

    @pl.loop(1, ROW)
    def _(k):
        other = lax.rem(row + k, ROW)
        pltpu.make_async_remote_copy(
            src_ref=send.at[other], dst_ref=recv.at[row], send_sem=sum_send, recv_sem=sum_recv,
            device_id=(other, feat), device_id_type=MESH).start()

    recv[row] = send[row]
    others = recv.at[pl.ds(0, ROW - 1)]
    pltpu.make_async_copy(others, others, sum_recv).wait()
    total = jnp.sum(recv[...], axis=0)

    grad_cum = total[:, 0:32]
    hess_cum = total[:, 32:64]
    grad_col = total[:, 64:96]
    hess_col = total[:, 96:128]
    grad_end = total[:, 31:32]
    hess_end = total[:, 63:64]
    grad_all = total[:, 95:96]
    hess_all = total[:, 127:128]
    quad_grad = (grad_cum, grad_end - grad_cum, grad_col - grad_cum, grad_all - grad_end - grad_col + grad_cum)
    quad_hess = (hess_cum, hess_end - hess_cum, hess_col - hess_cum, hess_all - hess_end - hess_col + hess_cum)
    gain = -(grad_all * grad_all) / (hess_all + LAMBDA_REG)
    for grad_part, hess_part in zip(quad_grad, quad_hess):
        gain = gain + grad_part * grad_part / (hess_part + LAMBDA_REG)
    tile = jnp.concatenate([gain, gain, gain, gain], axis=1)
    gains[feat] = tile

    @pl.loop(1, FEAT)
    def _(k):
        other = lax.rem(feat + k, FEAT)
        pltpu.make_async_remote_copy(
            src_ref=gains.at[feat], dst_ref=gains.at[feat], send_sem=gain_send, recv_sem=gain_recv,
            device_id=(row, other), device_id_type=MESH).start()

    others = gains.at[pl.ds(0, FEAT - 1)]
    pltpu.make_async_copy(others, others, gain_recv).wait()
    every = gains[...].reshape(FEAT * PAIRS, 128)
    top = jnp.max(every.T[0:32, :], axis=0, keepdims=True)
    top = jnp.concatenate([top, top], axis=1)
    peak[...] = top

    @pl.loop(1, ROW)
    def _(k):
        other = lax.rem(row + k, ROW)
        pltpu.make_async_remote_copy(
            src_ref=peak, dst_ref=peaks.at[row], send_sem=peak_send, recv_sem=peak_recv,
            device_id=(other, feat), device_id_type=MESH).start()

    table_ref[...] = jnp.dot(chosen, every, precision=lax.Precision.HIGHEST,
                             preferred_element_type=jnp.float32)[:, 0:32]
    peaks[row] = top
    others = peaks.at[pl.ds(0, ROW - 1)]
    pltpu.make_async_copy(others, others, peak_recv).wait()
    best_ref[...] = jnp.max(peaks[...], axis=0)[:, 0:64]

    sent = send.at[pl.ds(0, ROW - 1)]
    pltpu.make_async_copy(sent, sent, sum_send).wait()
    sent = gains.at[pl.ds(0, FEAT - 1)]
    pltpu.make_async_copy(sent, sent, gain_send).wait()
    sent = peaks.at[pl.ds(0, ROW - 1)]
    pltpu.make_async_copy(sent, sent, peak_send).wait()


def shards(bin_codes, gradients, hessians, pair_list, owners):
    rows = bin_codes.shape[1]
    vmem = pl.BlockSpec(memory_space=pltpu.VMEM)
    table, best = pl.pallas_call(
        kernel,
        out_shape=(jax.ShapeDtypeStruct((16, BINS), jnp.float32),
                   jax.ShapeDtypeStruct((1, FEAT * PAIRS), jnp.float32)),
        in_specs=[pl.BlockSpec(memory_space=pltpu.SMEM), vmem, vmem, vmem,
                  pl.BlockSpec(memory_space=pl.ANY)],
        out_specs=(vmem, vmem),
        scratch_shapes=[pltpu.VMEM((bin_codes.shape[0], rows // CHUNKS), jnp.int32)] * CHUNKS + [
            pltpu.VMEM((2, 128, 256), jnp.float32),
            pltpu.VMEM((ROW, PAIRS, 128), jnp.float32),
            pltpu.VMEM((ROW, PAIRS, 128), jnp.float32),
            pltpu.VMEM((FEAT, PAIRS, 128), jnp.float32),
            pltpu.VMEM((1, 128), jnp.float32),
            pltpu.VMEM((ROW, 1, 128), jnp.float32),
            pltpu.SemaphoreType.DMA((CHUNKS,)),
        ] + [pltpu.SemaphoreType.DMA] * 6,
        compiler_params=pltpu.CompilerParams(collective_id=0, has_side_effects=True),
    )(pair_list.T, owners.reshape(1, -1), gradients.reshape(rows // 128, 128),
      hessians.reshape(rows // 128, 128), bin_codes)
    return table, best.reshape(-1)


def solution(mesh):
    in_specs = (P(None, "row"), P("row"), P("row"), P(), P())
    out_specs = (P("feat", "row"), P())
    return jax.shard_map(shards, mesh=mesh, in_specs=in_specs, out_specs=out_specs, check_vma=False)
```

time: 291 us -> 33.2 us (0.11)
  waiting for transfers between devices: 147 us -> 0 us
  blocking collectives: 89.3 us -> 0 us
  Pallas kernels: 0 us -> 29.8 us
  other arithmetic: 20.2 us -> 0 us
  between operations: 14.9 us -> 0.64 us
  local copies, waits for them, and re-layouts: 11.4 us -> 2.43 us
  matrix products: 8.35 us -> 0 us
    psum x1 -> x0, waiting for transfers between devices: 147 us -> none  [shards(): summed = lax.psum(histogram, 'row')]
    pmax x1 -> x0, blocking collectives: 58.4 us -> none  [shards(): row_peak = lax.pmax(jnp.max(cut_gain, axis=1), 'row')]
    unnamed x1 -> x0, blocking collectives: 30.9 us -> none
    pallas_call x0 -> x1, Pallas kernels: none -> 29.8 us  [shards(): pl.pallas_call(kernel, out_shape=(jax.ShapeDtypeStruct((16, BINS), jnp.fl...]
    mul x1 -> x0, other arithmetic: 9.18 us -> none  [shards(): hot_second * gradients[None, None, :]]
    dot_general x1 -> x0, matrix products: 8.35 us -> none  [shards(): jnp.einsum('sar,sxr->sax', hot_first, weighted, preferred_element_type=jn...]
    another operation x2 -> x0, other arithmetic: 7.22 us -> none  [the longest x1 6.13 us: cumulate(): shaped = jnp.cumsum(shaped, axis=-1)]
    gather x4 -> x0, local copies, waits for them, and re-layouts: 7.21 us -> none  [the longest x2 5.36 us: shards(): picked = jnp.take(bin_codes, chosen_pairs.reshape(-1), axis=0)]
  transfers between devices with their start and end apart: 1 -> 0, of which waited for: 1 -> 0; matrix products, arithmetic and copies ran while one was open for 0% -> 0% of each run, Pallas kernels for 0% -> 0%
where the time goes in v1:
time: 33.2 us; the launch traced here: 32.9 us
  Pallas kernels  29.8 us (90%)
  local copies, waits for them, and re-layouts  2.43 us (7%)
  between operations  0.64 us (2%)
    pallas_call x1, Pallas kernels, shards(): pl.pallas_call(kernel, out_shape=(jax.ShapeDtypeStruct((16, BINS), jnp.fl...  29.8 us
    unnamed x2, local copies, waits for them, and re-layouts  2.43 us

profile of v1, /device:TPU:1, one launch (start us, length us, event | category | flops | bytes accessed | tf_op | source)
XLA Modules:
  0.0 32.9 jit_solution(12540910630547781294)
XLA Ops:
  0.6 29.8 %shard_map.68 = (f32[16,32]{1,0:T(8,128)}, f32[1,64]{1,0:T(1,128)}) custom-call(s32[2,64]{1,0:T(2,128)} %bitcast.7, s32[1,64]{1,0:T(1,128)} %bitcast.8, bf16[64,128]{1,0:T(8,128)(2,1)} %bitcast.5, bf16[64,128]{1,0:T(8,128)(2,1)} %bitcast.6, s32[256,8192]{1,0:T(8,128)} %codes_hbm.1), custom_call_target="tpu_custom_call" | custom-call | tf_op jit(solution)/shard_map/pallas_call | solution.py:171
  30.5 1.3 %copy.9 = f32[16,32]{1,0:T(8,128)} copy(f32[16,32]{1,0:T(8,128)} %get-tuple-element.8) | data formatting | bytes 4096
  31.8 1.1 %copy.10 = f32[64]{0:T(128)} copy(f32[64]{0:T(128)} %bitcast.9) | data formatting | bytes 512
